TPU v7x, 32 devices: a whole 2x2x4 slice. The times are simulated.
32 devices in a mesh: row: 16 (over z, y, x), col: 2 (over core).
Axes of the slice: x: 2, y: 2, z: 4, core: 2. Of those that a mesh axis runs over, the one named last changes fastest.
Arguments:
- vectors_in: bfloat16 [32768, 2048], P('row', 'col'), may hold values from -6 to 6
- panel: bfloat16 [32768, 256], P('row', 'col'), may hold values from -0.03125 to 0.03125
- factor: float32 [256, 256], replicated, may hold values from -3 to 8, as said below
- atom_basis: int32 [16, 128], P('row'), may hold values from 1 to 24, 2048 in all within a row
- proj_count: int32 [2048], P('row'), may hold values from 1 to 16
- coupling: bfloat16 [2048, 9, 384], P('row'), may hold values from -0.4375 to 0.4375
- block_present: int32 [2048, 9], P('row'), may hold values 0 or 1
- occ_mask: int32 [2048], P('col'), may hold values 0 or 1
- occ_weight: float32 [2048], P('col'), may hold values from 0.5 to 2
Outputs:
- vectors: bfloat16 [32768, 2048], P('row', 'col')
- density: float32 [2048, 256], P(('row', 'col'))
Inputs may be any that keep to these rules, and one draw needn't show every extreme that they name: `factor`: zero below the diagonal; the diagonal lies in 4 to 8. `atom_basis`: each row sums to 2048, and 24 is reached in each row.
All inputs are finite; a program needn't handle non-finite values. No bound on the sum of `block_present` or of `occ_mask` on one device may be relied on, other than what follows from the above.
Results may differ from a plain program's by a relative error of at most 0.0075.
Values may be sent and summed in bfloat16 or wider, within the bound.
A program may use at most 192 MiB of HBM per device.

v0:
```python
import jax
import jax.numpy as jnp
from jax import lax
from jax.sharding import PartitionSpec as P

NPMAX = 16
BMAX = 24
K = 9


def with_halo(array, sides, width):
    for axis, dim in sides:
        devices, length = (lax.axis_size(axis), array.shape[dim])
        up = [(i, (i + 1) % devices) for i in range(devices)]
        down = [(j, i) for i, j in up]
        last = lax.slice_in_dim(array, length - width, length, axis=dim)
        first = lax.slice_in_dim(array, 0, width, axis=dim)
        before = lax.ppermute(last, axis, up)
        after = lax.ppermute(first, axis, down)
        array = jnp.concatenate([before, array, after], axis=dim)
    return array


def panel_product(fragment, columns):
    return lax.dot_general(
        fragment, columns, (((0,), (0,)), ((), ())), preferred_element_type=jnp.float32
    )


def local(
    vectors_in, panel, factor, atom_basis, proj_count, coupling, block_present, occ_mask, occ_weight
):
    rows_here = vectors_in.shape[0]
    cols_here = vectors_in.shape[1]
    whole_panel = lax.all_gather(panel, "col", axis=1, tiled=True)
    inner_products = panel_product(whole_panel, vectors_in)
    inner_products = lax.psum(inner_products, "row")
    mixing = jnp.dot(factor.T, inner_products, precision=lax.Precision.HIGHEST).astype(jnp.bfloat16)
    update = jnp.dot(whole_panel, mixing, preferred_element_type=jnp.float32)
    vectors = (vectors_in.astype(jnp.float32) - update).astype(jnp.bfloat16)
    counts = atom_basis[0]
    atoms_here = counts.shape[0]
    starts = jnp.cumsum(counts) - counts
    slot_rank = jnp.arange(BMAX, dtype=jnp.int32)
    row_index = jnp.where(
        slot_rank[None, :] < counts[:, None], starts[:, None] + slot_rank[None, :], rows_here
    )
    padded = jnp.take(vectors, row_index.reshape(-1), axis=0, mode="fill", fill_value=0).reshape(
        atoms_here, BMAX, cols_here
    )
    rim_width = (K - 1) // 2
    extended = with_halo(padded, (("row", 0),), rim_width)
    projections = jnp.zeros((atoms_here, NPMAX, cols_here), jnp.float32)
    for relative in range(K):
        blocks = coupling[:, relative].reshape(atoms_here, NPMAX, BMAX)
        blocks = jnp.where(
            block_present[:, relative, None, None] > 0, blocks, jnp.zeros_like(blocks)
        )
        neighbours = extended[relative : relative + atoms_here]
        projections = projections + jnp.einsum(
            "aij,ajn->ain", blocks, neighbours, preferred_element_type=jnp.float32
        )
    kept_rows = (jnp.arange(NPMAX, dtype=jnp.int32)[None, :] < proj_count[:, None]).astype(
        jnp.float32
    )
    rounded = (projections * kept_rows[:, :, None]).astype(jnp.bfloat16)
    column_total = cols_here * lax.axis_size("col")
    weights = occ_mask.astype(jnp.float32) * occ_weight / column_total
    weighted = (rounded * weights[None, None, :]).astype(jnp.bfloat16)
    partial_value = jnp.einsum(
        "ain,ajn->aij", weighted, rounded, preferred_element_type=jnp.float32
    )
    partial_value = partial_value.reshape(atoms_here, NPMAX * NPMAX)
    density = lax.psum_scatter(
        partial_value.astype(jnp.bfloat16), "col", scatter_dimension=0, tiled=True
    ).astype(jnp.float32)
    return (vectors, density)


def solution(mesh):
    placed = (
        P("row", "col"),
        P("row", "col"),
        P(),
        P("row", None),
        P("row"),
        P("row", None, None),
        P("row", None),
        P("col"),
        P("col"),
    )
    return jax.shard_map(
        local,
        mesh=mesh,
        in_specs=placed,
        out_specs=(P("row", "col"), P(("row", "col"), None)),
        check_vma=False,
    )
```

profile of v0, /device:TPU:0, one launch (start us, length us, event | category | flops | bytes accessed | tf_op | source)
XLA Modules:
  0.0 292.0 jit_solution(12120854242485173018)
XLA Ops:
  7.2 0.7 all-gather.2.cloned.1.call-update
  8.0 0.8 copy.41
  8.7 0.2 reduce-window.8
  9.0 0.7 bitcast_subtract_fusion.1
  9.7 0.8 add_select_fusion
  10.6 1.4 fusion.48
  12.0 0.1 copy.67
  12.1 0.1 copy.68
  12.2 1.0 compare_bitcast_fusion.7
  13.3 0.4 copy.47
  13.7 6.5 %copy.39 = bf16[2048,1024]{0,1:T(8,128)(2,1)} copy(bf16[2048,1024]{1,0:T(8,128)(2,1)} %param.9) | data formatting | bytes 8388608 | tf_op args[0]
  20.3 0.1 copy.66
  20.5 1.2 copy.43
  21.7 1.2 copy.45
  22.9 0.4 copy.49
  23.3 0.1 copy.70
  23.5 0.1 copy.71
  23.6 1.2 copy.53
  24.8 1.2 copy.55
  26.1 0.1 copy.73
  26.3 1.2 copy.57
  27.5 0.4 copy.59
  28.1 0.4 copy.51
  28.7 4.8 %fusion.51 = f32[256,1024]{1,0:T(8,128)} fusion(bf16[2048,256]{1,0:T(8,128)(2,1)} %all-gather.2.cloned.1.call-done, bf16[2048,1024]{1,0:T(8,128)(2,1)} %param.9), kind=kOutput, calls=%fused_computation.88 | convolution fusion | flops 1073741824 | bytes 6291456 | tf_op jit(solution)/shard_map/dot_general | solution.py:25
  33.8 115.1 %all-reduce.2.cloned.1.call-done = f32[256,1024]{1,0:T(8,128)} async-done(((f32[256,1024]{1,0:T(8,128)}), f32[256,1024]{1,0:T(8,128)}) %all-reduce.2.cloned.1.call-update) | async-done | bytes 1048592 | tf_op jit(solution)/shard_map/psum | solution.py:37
  148.9 3.0 %convolution_convert_fusion = bf16[1024,256]{1,0:T(8,128)(2,1)S(1)} fusion(f32[256,1024]{1,0:T(8,128)} %all-reduce.2.cloned.1.call-done, f32[256,256]{1,0:T(8,128)S(1)} %copy-done), kind=kOutput, calls=%fused_computation.45 | convolution fusion | flops 805568512 | bytes 1835008 | tf_op jit(solution)/shard_map/dot_general | solution.py:38
  152.0 5.4 %fusion = bf16[2048,1024]{0,1:T(8,128)(2,1)} fusion(bf16[2048,1024]{0,1:T(8,128)(2,1)} %copy.39, bf16[1024,256]{1,0:T(8,128)(2,1)S(1)} %convolution_convert_fusion, bf16[2048,256]{1,0:T(8,128)(2,1)S(1)} %copy-done.4), kind=kOutput, calls=%fused_computation.8 | convolution fusion | flops 1080033280 | bytes 9961472 | tf_op jit(solution)/shard_map/dot_general | solution.py:39
  157.4 6.4 %copy.61 = bf16[2048,1024]{1,0:T(8,128)(2,1)} copy(bf16[2048,1024]{0,1:T(8,128)(2,1)} %fusion) | data formatting | bytes 8388608
  163.8 18.7 %gather_fusion = bf16[3072,1024]{1,0:T(8,128)(2,1)} fusion(bf16[2048,1024]{1,0:T(8,128)(2,1)} %copy.61, s32[3072]{0:T(1024)S(1)} %broadcast_clamp_fusion), kind=kCustom, calls=%fused_computation | custom fusion | bytes 12595200 | tf_op jit(solution)/shard_map/jit(_take)/gather | solution.py:48
  182.4 4.1 %broadcast_select_fusion = bf16[3072,1024]{1,0:T(8,128)(2,1)S(1)} fusion(bf16[3072,1024]{1,0:T(8,128)(2,1)} %gather_fusion, pred[3072]{0:T(1024)(128)(4,1)S(1)} %compare_and_fusion.1), kind=kLoop, calls=%fused_computation.36 | loop fusion | flops 3145728 | bytes 12585984 | tf_op jit(solution)/shard_map/jit(_take)/select_n | solution.py:48
  186.5 1.5 collective-permute-start
  188.1 4.1 %collective-permute-start.1 = (bf16[4,24,1024]{2,1,0:T(8,128)(2,1)S(1)}, bf16[4,24,1024]{2,1,0:T(8,128)(2,1)S(1)}, u32[]{:S(2)}, u32[]{:S(2)}) collective-permute-start(bf16[4,24,1024]{2,1,0:T(8,128)(2,1)S(1)} %bitcast.69), channel_id=1, source_target_pairs={{2,0},{4,2},{6,4},{8,6},{10,8},{12,10},{14,12},{16,14},{18,16},{20... | collective-permute-start | bytes 589832 | tf_op jit(solution)/shard_map/ppermute | solution.py:19
  192.2 0.7 broadcast_select_fusion.1
  193.0 2.9 collective-permute-done
  195.9 4.3 %fusion.12 = f32[128,16,1024]{2,1,0:T(8,128)} fusion(bf16[128,16,24]{2,1,0:T(8,128)(2,1)S(1)} %copy.47, bf16[4,24,1024]{2,1,0:T(8,128)(2,1)S(1)} %collective-permute-done, bf16[128,24,1024]{2,1,0:T(8,128)(2,1)S(1)} %broadcast_select_fusion.1), kind=kOutput, calls=%fused_computation.19 | convolution fusion | flops 103809024 | bytes 14974976 | tf_op jit(solution)/shard_map/aij,ajn->ain/dot_general | solution.py:60
  200.2 4.3 %fusion.15 = f32[128,16,1024]{2,1,0:T(8,128)} fusion(bf16[128,16,24]{2,1,0:T(8,128)(2,1)S(1)} %copy-done.5, bf16[4,24,1024]{2,1,0:T(8,128)(2,1)S(1)} %collective-permute-done, bf16[128,24,1024]{2,1,0:T(8,128)(2,1)S(1)} %broadcast_select_fusion.1), kind=kOutput, calls=%fused_computation.21 | convolution fusion | flops 103809024 | bytes 14974976 | tf_op jit(solution)/shard_map/aij,ajn->ain/dot_general | solution.py:60
  204.4 4.3 %fusion.18 = f32[128,16,1024]{2,1,0:T(8,128)} fusion(bf16[128,16,24]{2,1,0:T(8,128)(2,1)S(1)} %copy-done.6, bf16[4,24,1024]{2,1,0:T(8,128)(2,1)S(1)} %collective-permute-done, bf16[128,24,1024]{2,1,0:T(8,128)(2,1)S(1)} %broadcast_select_fusion.1), kind=kOutput, calls=%fused_computation.23 | convolution fusion | flops 103809024 | bytes 14974976 | tf_op jit(solution)/shard_map/aij,ajn->ain/dot_general | solution.py:60
  208.8 4.3 %fusion.25 = f32[128,16,1024]{2,1,0:T(8,128)} fusion(bf16[128,16,24]{2,1,0:T(8,128)(2,1)S(1)} %copy.49, bf16[128,24,1024]{2,1,0:T(8,128)(2,1)S(1)} %broadcast_select_fusion.1, bf16[4,24,1024]{2,1,0:T(8,128)(2,1)S(1)} %collective-permute-done), kind=kOutput, calls=%fused_computation.31 | convolution fusion | flops 103809024 | bytes 14974976 | tf_op jit(solution)/shard_map/aij,ajn->ain/dot_general | solution.py:60
  213.1 4.3 %fusion.6 = f32[128,16,1024]{2,1,0:T(8,128)} fusion(bf16[128,16,24]{2,1,0:T(8,128)(2,1)S(1)} %copy-done.7, bf16[4,24,1024]{2,1,0:T(8,128)(2,1)S(1)} %collective-permute-done.1, bf16[128,24,1024]{2,1,0:T(8,128)(2,1)S(1)} %broadcast_select_fusion.1), kind=kOutput, calls=%fused_computation.15 | convolution fusion | flops 103809024 | bytes 14974976 | tf_op jit(solution)/shard_map/aij,ajn->ain/dot_general | solution.py:60
  217.4 4.3 %fusion.9 = f32[128,16,1024]{2,1,0:T(8,128)} fusion(bf16[128,16,24]{2,1,0:T(8,128)(2,1)S(1)} %copy-done.8, bf16[4,24,1024]{2,1,0:T(8,128)(2,1)S(1)} %collective-permute-done.1, bf16[128,24,1024]{2,1,0:T(8,128)(2,1)S(1)} %broadcast_select_fusion.1), kind=kOutput, calls=%fused_computation.17 | convolution fusion | flops 103809024 | bytes 14974976 | tf_op jit(solution)/shard_map/aij,ajn->ain/dot_general | solution.py:60
  221.6 4.3 %fusion.3 = f32[128,16,1024]{2,1,0:T(8,128)} fusion(bf16[128,16,24]{2,1,0:T(8,128)(2,1)S(1)} %copy-done.9, bf16[4,24,1024]{2,1,0:T(8,128)(2,1)S(1)} %collective-permute-done.1, bf16[128,24,1024]{2,1,0:T(8,128)(2,1)S(1)} %broadcast_select_fusion.1), kind=kOutput, calls=%fused_computation.13 | convolution fusion | flops 103809024 | bytes 14974976 | tf_op jit(solution)/shard_map/aij,ajn->ain/dot_general | solution.py:60
  225.9 4.3 %fusion.20 = f32[128,16,1024]{2,1,0:T(8,128)} fusion(bf16[128,16,24]{2,1,0:T(8,128)(2,1)S(1)} %copy.59, bf16[4,24,1024]{2,1,0:T(8,128)(2,1)S(1)} %collective-permute-done.1, bf16[128,24,1024]{2,1,0:T(8,128)(2,1)S(1)} %broadcast_select_fusion.1), kind=kOutput, calls=%fused_computation.25 | convolution fusion | flops 103809024 | bytes 14974976 | tf_op jit(solution)/shard_map/aij,ajn->ain/dot_general | solution.py:60
  230.2 46.4 %fusion.37 = bf16[128,16,16]{2,1,0:T(8,128)(2,1)S(1)} fusion(f32[128,16,1024]{2,1,0:T(8,128)} %fusion.20, f32[128,16,1024]{2,1,0:T(8,128)} %fusion.3, f32[128,16,1024]{2,1,0:T(8,128)} %fusion.9, f32[128,16,1024]{2,1,0:T(8,128)} %fusion.6, f32[128,16,1024]{2,1,0:T(8,128)} %fusion.25, f32[128,16,1024]{2,1,0:T(8,128)} %fusion.12, ...), kind=kOutput, calls=%fused_computation.46 | convolution fusion | flops 316702720 | bytes 73576448 | tf_op jit(solution)/shard_map/ain,ajn->aij/dot_general | solution.py:70
  276.6 0.4 copy.60
  277.0 0.7 copy.63
  277.8 6.1 %reduce-scatter.4.cloned.1.call-done = bf16[64,256]{1,0:T(8,128)(2,1)} async-done(((bf16[128,256]{1,0:T(8,128)(2,1)}), bf16[64,256]{1,0:T(8,128)(2,1)}) %reduce-scatter.4.cloned.1.call-update) | async-done | bytes 32784
  283.9 0.9 copy.64
  284.7 0.7 copy.62
  (53 shorter events, 1.3 us)
Async XLA Ops:
  7.2 141.7 %copy-start = (f32[256,256]{1,0:T(8,128)S(1)}, f32[256,256]{1,0:T(8,128)}, u32[]{:S(2)}) copy-start(f32[256,256]{1,0:T(8,128)} %param.11) | copy-start | bytes 786436
  7.2 21.5 %all-gather.2.cloned.1.call-start = ((), (), s32[]{:S(2)}) async-start(), calls=%async_computation.1 | async-start | bytes 1572864 | tf_op jit(solution)/shard_map/all_gather | solution.py:35
  7.9 141.0 %all-reduce.2.cloned.1.call-start = ((), (), s32[]{:S(2)}) async-start(), calls=%async_computation.2 | async-start | bytes 2097152 | tf_op jit(solution)/shard_map/psum | solution.py:37
  13.7 14.8 %copy-start.11 = (f32[1024]{0:T(1024)S(1)}, f32[1024]{0:T(1024)}, u32[]{:S(2)}) copy-start(f32[1024]{0:T(1024)} %param.17) | copy-start | bytes 12292
  13.7 14.8 %copy-start.12 = (s32[1024]{0:T(1024)S(1)}, s32[1024]{0:T(1024)}, u32[]{:S(2)}) copy-start(s32[1024]{0:T(1024)} %param.16) | copy-start | bytes 12292
  13.7 14.8 %copy-start.10 = (s32[1,128]{1,0:T(1,128)S(1)}, s32[1,128]{1,0:T(1,128)}, u32[]{:S(2)}) copy-start(s32[1,128]{1,0:T(1,128)} %param.12) | copy-start | bytes 1540
  24.8 8.8 %copy-start.13 = (s32[128]{0:T(128)S(1)}, s32[128]{0:T(128)}, u32[]{:S(2)}) copy-start(s32[128]{0:T(128)} %param.13) | copy-start | bytes 1540
  28.7 123.2 %copy-start.4 = (bf16[2048,256]{1,0:T(8,128)(2,1)S(1)}, bf16[2048,256]{1,0:T(8,128)(2,1)}, u32[]{:S(2)}) copy-start(bf16[2048,256]{1,0:T(8,128)(2,1)} %all-gather.2.cloned.1.call-done) | copy-start | bytes 3145732
  33.6 250.3 %reduce-scatter.4.cloned.1.call-start = ((), (), s32[]{:S(2)}) async-start(), calls=%async_computation.3 | async-start | bytes 98304
  182.4 9.8 %copy-start.3 = (bf16[3072,1024]{1,0:T(8,128)(2,1)S(1)}, bf16[3072,1024]{1,0:T(8,128)(2,1)}, u32[]{:S(2)}) copy-start(bf16[3072,1024]{1,0:T(8,128)(2,1)} %gather_fusion) | copy-start | bytes 18874372
  186.5 9.3 %collective-permute-start = (bf16[4,24,1024]{2,1,0:T(8,128)(2,1)S(1)}, bf16[4,24,1024]{2,1,0:T(8,128)(2,1)S(1)}, u32[]{:S(2)}, u32[]{:S(2)}) collective-permute-start(bf16[4,24,1024]{2,1,0:T(8,128)(2,1)S(1)} %bitcast.70), channel_id=1, source_target_pairs={{0,2},{2,4},{4,6},{6,8},{8,10},{10,12},{12,14},{14,16},{16,18},{18... | collective-permute-start | bytes 589832 | tf_op jit(solution)/shard_map/ppermute | solution.py:18
  188.1 25.0 %collective-permute-start.1 = (bf16[4,24,1024]{2,1,0:T(8,128)(2,1)S(1)}, bf16[4,24,1024]{2,1,0:T(8,128)(2,1)S(1)}, u32[]{:S(2)}, u32[]{:S(2)}) collective-permute-start(bf16[4,24,1024]{2,1,0:T(8,128)(2,1)S(1)} %bitcast.69), channel_id=1, source_target_pairs={{2,0},{4,2},{6,4},{8,6},{10,8},{12,10},{14,12},{16,14},{18,16},{20... | collective-permute-start | bytes 589832 | tf_op jit(solution)/shard_map/ppermute | solution.py:19
  192.9 33.0 %copy-start.2 = (bf16[128,24,1024]{2,1,0:T(8,128)(2,1)}, bf16[128,24,1024]{2,1,0:T(8,128)(2,1)S(1)}, u32[]{:S(2)}) copy-start(bf16[128,24,1024]{2,1,0:T(8,128)(2,1)S(1)} %broadcast_select_fusion.1) | copy-start | bytes 18874372
  193.0 7.2 %copy-start.5 = (bf16[128,16,24]{2,1,0:T(8,128)(2,1)S(1)}, bf16[128,16,24]{2,1,0:T(8,128)(2,1)}, u32[]{:S(2)}) copy-start(bf16[128,16,24]{2,1,0:T(8,128)(2,1)} %copy.43) | copy-start | bytes 294916
  200.2 4.3 %copy-start.6 = (bf16[128,16,24]{2,1,0:T(8,128)(2,1)S(1)}, bf16[128,16,24]{2,1,0:T(8,128)(2,1)}, u32[]{:S(2)}) copy-start(bf16[128,16,24]{2,1,0:T(8,128)(2,1)} %copy.45) | copy-start | bytes 294916
  208.8 4.3 %copy-start.7 = (bf16[128,16,24]{2,1,0:T(8,128)(2,1)S(1)}, bf16[128,16,24]{2,1,0:T(8,128)(2,1)}, u32[]{:S(2)}) copy-start(bf16[128,16,24]{2,1,0:T(8,128)(2,1)} %copy.53) | copy-start | bytes 294916
  213.1 4.3 %copy-start.8 = (bf16[128,16,24]{2,1,0:T(8,128)(2,1)S(1)}, bf16[128,16,24]{2,1,0:T(8,128)(2,1)}, u32[]{:S(2)}) copy-start(bf16[128,16,24]{2,1,0:T(8,128)(2,1)} %copy.55) | copy-start | bytes 294916
  217.4 4.3 %copy-start.9 = (bf16[128,16,24]{2,1,0:T(8,128)(2,1)S(1)}, bf16[128,16,24]{2,1,0:T(8,128)(2,1)}, u32[]{:S(2)}) copy-start(bf16[128,16,24]{2,1,0:T(8,128)(2,1)} %copy.57) | copy-start | bytes 294916
  230.2 55.2 %copy-start.1 = (f32[256,256]{1,0:T(8,128)S(1)}, f32[256,256]{1,0:T(8,128)}, u32[]{:S(2)}) copy-start(f32[256,256]{1,0:T(8,128)} %param.11) | copy-start | bytes 786436
Sparse Core Ops, SparseCore 0:
  9.5 11.4 all-gather.1
  33.7 115.1 all-reduce.1
  277.9 5.9 reduce-scatter.3
where the time goes:
time: 293 us; the launch traced here: 292 us
  waiting for transfers between devices  125 us (43%)
  matrix products  94 us (32%)
  local copies, waits for them, and re-layouts  45.5 us (16%)
  between operations  14.1 us (5%)
  other arithmetic  7.78 us (3%)
  starting transfers between devices  5.79 us (2%)
    psum x1, waiting for transfers between devices, local(): inner_products = lax.psum(inner_products, 'row')  115 us
    dot_general x1, matrix products, local(): jnp.einsum('ain,ajn->aij', weighted, rounded, preferred_element_type=jnp....  46.4 us
    dot_general x8, matrix products, local(): jnp.einsum('aij,ajn->ain', blocks, neighbours, preferred_element_type=jnp...  34.3 us
    gather x1, local copies, waits for them, and re-layouts, local(): jnp.take(vectors, row_index.reshape(-1), axis=0, mode='fill', fill_value=0)  18.7 us
    unnamed x42, local copies, waits for them, and re-layouts  16.4 us
    select_n x9, local copies, waits for them, and re-layouts, local(): jnp.where(block_present[:, relative, None, None] > 0, blocks, jnp.zeros_l...  7.69 us
    unnamed x4, waiting for transfers between devices  6.78 us
  transfers between devices with their start and end apart: 5, of which 3 were waited for; matrix products, arithmetic and copies ran while one was open for 13% of the time, Pallas kernels for 0%

commit v1 on v0

--- a/solution.py
+++ b/solution.py
@@ -34,7 +34,7 @@
     cols_here = vectors_in.shape[1]
     whole_panel = lax.all_gather(panel, "col", axis=1, tiled=True)
     inner_products = panel_product(whole_panel, vectors_in)
-    inner_products = lax.psum(inner_products, "row")
+    inner_products = jnp.sum(lax.all_gather(inner_products, "row"), axis=0)
     mixing = jnp.dot(factor.T, inner_products, precision=lax.Precision.HIGHEST).astype(jnp.bfloat16)
     update = jnp.dot(whole_panel, mixing, preferred_element_type=jnp.float32)
     vectors = (vectors_in.astype(jnp.float32) - update).astype(jnp.bfloat16)

time: 293 us -> 369 us (1.26)
  waiting for transfers between devices: 125 us -> 199 us
  other arithmetic: 7.78 us -> 13.3 us
    all_gather x0 -> x1, waiting for transfers between devices: none -> 176 us  [local(): inner_products = jnp.sum(lax.all_gather(inner_products, 'row'), axis=0)]
    psum x1 -> x0, waiting for transfers between devices: 115 us -> none  [local(): inner_products = lax.psum(inner_products, 'row')]
    all_gather x1, waiting for transfers between devices: 0.02 us -> 13.1 us  [local(): whole_panel = lax.all_gather(panel, 'col', axis=1, tiled=True)]
    reduce_sum x0 -> x1, other arithmetic: none -> 7.75 us  [local(): inner_products = jnp.sum(lax.all_gather(inner_products, 'row'), axis=0)]
    unnamed x42 -> x44, local copies, waits for them, and re-layouts: 16.4 us -> 16.4 us
  transfers between devices with their start and end apart: 5 -> 5, of which waited for: 3 -> 4; matrix products, arithmetic and copies ran while one was open for 13% -> 9% of each run, Pallas kernels for 0% -> 0%
where the time goes in v1:
time: 369 us
  waiting for transfers between devices  199 us (54%)
  matrix products  93 us (25%)
  local copies, waits for them, and re-layouts  43.5 us (12%)
  between operations  14.1 us (4%)
  other arithmetic  13.3 us (4%)
  starting transfers between devices  5.79 us (2%)
    all_gather x1, waiting for transfers between devices, local(): inner_products = jnp.sum(lax.all_gather(inner_products, 'row'), axis=0)  176 us
    dot_general x1, matrix products, local(): jnp.einsum('ain,ajn->aij', weighted, rounded, preferred_element_type=jnp....  46.4 us
    dot_general x8, matrix products, local(): jnp.einsum('aij,ajn->ain', blocks, neighbours, preferred_element_type=jnp...  34.3 us
    gather x1, local copies, waits for them, and re-layouts, local(): jnp.take(vectors, row_index.reshape(-1), axis=0, mode='fill', fill_value=0)  18.6 us
    unnamed x44, local copies, waits for them, and re-layouts  16.4 us
    all_gather x1, waiting for transfers between devices, local(): whole_panel = lax.all_gather(panel, 'col', axis=1, tiled=True)  13.1 us
    reduce_sum x1, other arithmetic, local(): inner_products = jnp.sum(lax.all_gather(inner_products, 'row'), axis=0)  7.75 us
    select_n x9, local copies, waits for them, and re-layouts, local(): jnp.where(block_present[:, relative, None, None] > 0, blocks, jnp.zeros_l...  7.69 us
  transfers between devices with their start and end apart: 5, of which 4 were waited for; matrix products, arithmetic and copies ran while one was open for 9% of the time, Pallas kernels for 0%

profile of v1, /device:TPU:0, one launch (start us, length us, event | category | flops | bytes accessed | tf_op | source)
XLA Modules:
  0.0 368.7 jit_solution(13064107049780307365)
XLA Ops:
  7.2 0.7 all-gather.4.cloned.1.call-update
  8.0 13.1 %all-gather.4.cloned.1.call-done = bf16[2048,256]{1,0:T(8,128)(2,1)} async-done(((bf16[2048,128]{1,0:T(8,128)(2,1)}), bf16[2048,256]{1,0:T(8,128)(2,1)}) %all-gather.4.cloned.1.call-update) | async-done | bytes 1048592 | tf_op jit(solution)/shard_map/all_gather | solution.py:35
  21.1 4.8 %fusion.51 = f32[256,1024]{1,0:T(8,128)} fusion(bf16[2048,256]{1,0:T(8,128)(2,1)} %all-gather.4.cloned.1.call-done, bf16[2048,1024]{1,0:T(8,128)(2,1)} %param.9), kind=kOutput, calls=%fused_computation.88 | convolution fusion | flops 1073741824 | bytes 6291456 | tf_op jit(solution)/shard_map/dot_general | solution.py:25
  25.9 6.5 %copy.39 = bf16[2048,1024]{0,1:T(8,128)(2,1)} copy(bf16[2048,1024]{1,0:T(8,128)(2,1)} %param.9) | data formatting | bytes 8388608 | tf_op args[0]
  32.5 0.2 reduce-window.8
  33.2 0.1 copy.67
  33.4 0.1 copy.68
  33.6 0.4 copy.47
  34.0 0.1 copy.66
  34.1 0.1 copy.65
  34.3 1.2 copy.43
  35.5 1.2 copy.45
  36.7 0.4 copy.49
  37.1 0.1 copy.70
  37.2 0.1 copy.71
  37.4 1.2 copy.53
  38.6 1.2 copy.55
  39.8 0.1 copy.72
  39.9 0.1 copy.73
  40.1 1.2 copy.57
  41.3 0.4 copy.59
  41.7 0.1 copy.69
  41.8 0.4 copy.51
  42.6 175.6 %all-gather.6.cloned.1.call-done = f32[4096,1024]{1,0:T(8,128)} async-done(((f32[256,1024]{1,0:T(8,128)}), f32[4096,1024]{1,0:T(8,128)}) %all-gather.6.cloned.1.call-update) | async-done | bytes 16777232 | tf_op jit(solution)/shard_map/all_gather | solution.py:37
  218.2 7.7 %reduce_sum.9 = f32[256,1024]{1,0:T(8,128)S(1)} reduce(f32[16,256,1024]{2,1,0:T(8,128)} %bitcast.60, f32[]{:T(128)} %constant.10.clone.1), dimensions={0}, to_apply=%region_0.0 | reduce | flops 3932160 | bytes 17825796 | tf_op jit(solution)/shard_map/reduce_sum | solution.py:37
  226.0 1.8 convolution_convert_fusion
  227.8 5.8 %fusion = bf16[2048,1024]{0,1:T(8,128)(2,1)} fusion(bf16[2048,1024]{0,1:T(8,128)(2,1)} %copy.39, bf16[1024,256]{1,0:T(8,128)(2,1)S(1)} %convolution_convert_fusion, bf16[2048,256]{1,0:T(8,128)(2,1)} %all-gather.4.cloned.1.call-done), kind=kOutput, calls=%fused_computation.8 | convolution fusion | flops 1080033280 | bytes 9961472 | tf_op jit(solution)/shard_map/dot_general | solution.py:39
  233.5 6.4 %copy.61 = bf16[2048,1024]{1,0:T(8,128)(2,1)} copy(bf16[2048,1024]{0,1:T(8,128)(2,1)} %fusion) | data formatting | bytes 8388608
  239.9 18.6 %gather_fusion = bf16[3072,1024]{1,0:T(8,128)(2,1)} fusion(bf16[2048,1024]{1,0:T(8,128)(2,1)} %copy.61, s32[3072]{0:T(1024)S(1)} %broadcast_clamp_fusion), kind=kCustom, calls=%fused_computation | custom fusion | bytes 12595200 | tf_op jit(solution)/shard_map/jit(_take)/gather | solution.py:48
  258.5 4.1 %broadcast_select_fusion = bf16[3072,1024]{1,0:T(8,128)(2,1)S(1)} fusion(bf16[3072,1024]{1,0:T(8,128)(2,1)} %gather_fusion, pred[3072]{0:T(1024)(128)(4,1)S(1)} %compare_and_fusion.1), kind=kLoop, calls=%fused_computation.36 | loop fusion | flops 3145728 | bytes 12585984 | tf_op jit(solution)/shard_map/jit(_take)/select_n | solution.py:48
  262.6 1.5 collective-permute-start
  264.1 4.2 %collective-permute-start.1 = (bf16[4,24,1024]{2,1,0:T(8,128)(2,1)S(1)}, bf16[4,24,1024]{2,1,0:T(8,128)(2,1)S(1)}, u32[]{:S(2)}, u32[]{:S(2)}) collective-permute-start(bf16[4,24,1024]{2,1,0:T(8,128)(2,1)S(1)} %bitcast.71), channel_id=1, source_target_pairs={{2,0},{4,2},{6,4},{8,6},{10,8},{12,10},{14,12},{16,14},{18,16},{20... | collective-permute-start | bytes 589832 | tf_op jit(solution)/shard_map/ppermute | solution.py:19
  268.3 0.7 broadcast_select_fusion.1
  269.0 3.3 collective-permute-done
  272.3 4.3 %fusion.12 = f32[128,16,1024]{2,1,0:T(8,128)} fusion(bf16[128,16,24]{2,1,0:T(8,128)(2,1)S(1)} %copy.47, bf16[4,24,1024]{2,1,0:T(8,128)(2,1)S(1)} %collective-permute-done, bf16[128,24,1024]{2,1,0:T(8,128)(2,1)S(1)} %broadcast_select_fusion.1), kind=kOutput, calls=%fused_computation.19 | convolution fusion | flops 103809024 | bytes 14974976 | tf_op jit(solution)/shard_map/aij,ajn->ain/dot_general | solution.py:60
  276.6 4.2 %fusion.15 = f32[128,16,1024]{2,1,0:T(8,128)} fusion(bf16[128,16,24]{2,1,0:T(8,128)(2,1)S(1)} %copy-done.5, bf16[4,24,1024]{2,1,0:T(8,128)(2,1)S(1)} %collective-permute-done, bf16[128,24,1024]{2,1,0:T(8,128)(2,1)S(1)} %broadcast_select_fusion.1), kind=kOutput, calls=%fused_computation.21 | convolution fusion | flops 103809024 | bytes 14974976 | tf_op jit(solution)/shard_map/aij,ajn->ain/dot_general | solution.py:60
  280.8 4.3 %fusion.18 = f32[128,16,1024]{2,1,0:T(8,128)} fusion(bf16[128,16,24]{2,1,0:T(8,128)(2,1)S(1)} %copy-done.6, bf16[4,24,1024]{2,1,0:T(8,128)(2,1)S(1)} %collective-permute-done, bf16[128,24,1024]{2,1,0:T(8,128)(2,1)S(1)} %broadcast_select_fusion.1), kind=kOutput, calls=%fused_computation.23 | convolution fusion | flops 103809024 | bytes 14974976 | tf_op jit(solution)/shard_map/aij,ajn->ain/dot_general | solution.py:60
  285.1 4.3 %fusion.25 = f32[128,16,1024]{2,1,0:T(8,128)} fusion(bf16[128,16,24]{2,1,0:T(8,128)(2,1)S(1)} %copy.49, bf16[128,24,1024]{2,1,0:T(8,128)(2,1)S(1)} %broadcast_select_fusion.1, bf16[4,24,1024]{2,1,0:T(8,128)(2,1)S(1)} %collective-permute-done), kind=kOutput, calls=%fused_computation.31 | convolution fusion | flops 103809024 | bytes 14974976 | tf_op jit(solution)/shard_map/aij,ajn->ain/dot_general | solution.py:60
  289.5 4.3 %fusion.6 = f32[128,16,1024]{2,1,0:T(8,128)} fusion(bf16[128,16,24]{2,1,0:T(8,128)(2,1)S(1)} %copy-done.7, bf16[4,24,1024]{2,1,0:T(8,128)(2,1)S(1)} %collective-permute-done.1, bf16[128,24,1024]{2,1,0:T(8,128)(2,1)S(1)} %broadcast_select_fusion.1), kind=kOutput, calls=%fused_computation.15 | convolution fusion | flops 103809024 | bytes 14974976 | tf_op jit(solution)/shard_map/aij,ajn->ain/dot_general | solution.py:60
  293.8 4.3 %fusion.9 = f32[128,16,1024]{2,1,0:T(8,128)} fusion(bf16[128,16,24]{2,1,0:T(8,128)(2,1)S(1)} %copy-done.8, bf16[4,24,1024]{2,1,0:T(8,128)(2,1)S(1)} %collective-permute-done.1, bf16[128,24,1024]{2,1,0:T(8,128)(2,1)S(1)} %broadcast_select_fusion.1), kind=kOutput, calls=%fused_computation.17 | convolution fusion | flops 103809024 | bytes 14974976 | tf_op jit(solution)/shard_map/aij,ajn->ain/dot_general | solution.py:60
  298.0 4.3 %fusion.3 = f32[128,16,1024]{2,1,0:T(8,128)} fusion(bf16[128,16,24]{2,1,0:T(8,128)(2,1)S(1)} %copy-done.9, bf16[4,24,1024]{2,1,0:T(8,128)(2,1)S(1)} %collective-permute-done.1, bf16[128,24,1024]{2,1,0:T(8,128)(2,1)S(1)} %broadcast_select_fusion.1), kind=kOutput, calls=%fused_computation.13 | convolution fusion | flops 103809024 | bytes 14974976 | tf_op jit(solution)/shard_map/aij,ajn->ain/dot_general | solution.py:60
  302.3 4.3 %fusion.20 = f32[128,16,1024]{2,1,0:T(8,128)} fusion(bf16[128,16,24]{2,1,0:T(8,128)(2,1)S(1)} %copy.59, bf16[4,24,1024]{2,1,0:T(8,128)(2,1)S(1)} %collective-permute-done.1, bf16[128,24,1024]{2,1,0:T(8,128)(2,1)S(1)} %broadcast_select_fusion.1), kind=kOutput, calls=%fused_computation.25 | convolution fusion | flops 103809024 | bytes 14974976 | tf_op jit(solution)/shard_map/aij,ajn->ain/dot_general | solution.py:60
  306.6 46.4 %fusion.37 = bf16[128,16,16]{2,1,0:T(8,128)(2,1)S(1)} fusion(f32[128,16,1024]{2,1,0:T(8,128)} %fusion.20, f32[128,16,1024]{2,1,0:T(8,128)} %fusion.3, f32[128,16,1024]{2,1,0:T(8,128)} %fusion.9, f32[128,16,1024]{2,1,0:T(8,128)} %fusion.6, f32[128,16,1024]{2,1,0:T(8,128)} %fusion.25, f32[128,16,1024]{2,1,0:T(8,128)} %fusion.12, ...), kind=kOutput, calls=%fused_computation.46 | convolution fusion | flops 316702720 | bytes 73576448 | tf_op jit(solution)/shard_map/ain,ajn->aij/dot_general | solution.py:70
  353.0 0.4 copy.60
  353.4 0.7 copy.63
  354.2 6.3 %reduce-scatter.4.cloned.1.call-done = bf16[64,256]{1,0:T(8,128)(2,1)} async-done(((bf16[128,256]{1,0:T(8,128)(2,1)}), bf16[64,256]{1,0:T(8,128)(2,1)}) %reduce-scatter.4.cloned.1.call-update) | async-done | bytes 32784
  360.5 0.9 copy.64
  361.4 0.7 copy.62
  (56 shorter events, 1.2 us)
Async XLA Ops:
  7.2 218.8 %copy-start = (f32[256,256]{1,0:T(8,128)S(1)}, f32[256,256]{1,0:T(8,128)}, u32[]{:S(2)}) copy-start(f32[256,256]{1,0:T(8,128)} %param.11) | copy-start | bytes 786436
  7.2 13.9 %all-gather.4.cloned.1.call-start = ((), (), s32[]{:S(2)}) async-start(), calls=%async_computation.1 | async-start | bytes 1572864 | tf_op jit(solution)/shard_map/all_gather | solution.py:35
  7.9 210.3 %all-gather.6.cloned.1.call-start = ((), (), s32[]{:S(2)}) async-start(), calls=%async_computation.2 | async-start | bytes 17825792 | tf_op jit(solution)/shard_map/all_gather | solution.py:37
  25.8 6.6 %copy-start.10 = (s32[1,128]{1,0:T(1,128)S(1)}, s32[1,128]{1,0:T(1,128)}, u32[]{:S(2)}) copy-start(s32[1,128]{1,0:T(1,128)} %param.12) | copy-start | bytes 1540
  25.8 7.3 %copy-start.4 = (bf16[128,9,384]{2,0,1:T(8,128)(2,1)S(1)}, bf16[128,9,384]{2,0,1:T(8,128)(2,1)}, u32[]{:S(2)}) copy-start(bf16[128,9,384]{2,0,1:T(8,128)(2,1)} %param.14) | copy-start | bytes 2654212
  25.8 7.7 %copy-start.13 = (s32[128,9]{0,1:T(8,128)S(1)}, s32[128,9]{0,1:T(8,128)}, u32[]{:S(2)}) copy-start(s32[128,9]{0,1:T(8,128)} %param.15) | copy-start | bytes 13828
  25.8 334.7 %reduce-scatter.4.cloned.1.call-start = ((), (), s32[]{:S(2)}) async-start(), calls=%async_computation.3 | async-start | bytes 98304
  32.4 9.9 %copy-start.11 = (f32[1024]{0:T(1024)S(1)}, f32[1024]{0:T(1024)}, u32[]{:S(2)}) copy-start(f32[1024]{0:T(1024)} %param.17) | copy-start | bytes 12292
  32.4 9.9 %copy-start.12 = (s32[1024]{0:T(1024)S(1)}, s32[1024]{0:T(1024)}, u32[]{:S(2)}) copy-start(s32[1024]{0:T(1024)} %param.16) | copy-start | bytes 12292
  32.4 10.1 %copy-start.14 = (s32[128]{0:T(128)S(1)}, s32[128]{0:T(128)}, u32[]{:S(2)}) copy-start(s32[128]{0:T(128)} %param.13) | copy-start | bytes 1540
  258.5 9.8 %copy-start.3 = (bf16[3072,1024]{1,0:T(8,128)(2,1)S(1)}, bf16[3072,1024]{1,0:T(8,128)(2,1)}, u32[]{:S(2)}) copy-start(bf16[3072,1024]{1,0:T(8,128)(2,1)} %gather_fusion) | copy-start | bytes 18874372
  262.6 9.7 %collective-permute-start = (bf16[4,24,1024]{2,1,0:T(8,128)(2,1)S(1)}, bf16[4,24,1024]{2,1,0:T(8,128)(2,1)S(1)}, u32[]{:S(2)}, u32[]{:S(2)}) collective-permute-start(bf16[4,24,1024]{2,1,0:T(8,128)(2,1)S(1)} %bitcast.72), channel_id=1, source_target_pairs={{0,2},{2,4},{4,6},{6,8},{8,10},{10,12},{12,14},{14,16},{16,18},{18... | collective-permute-start | bytes 589832 | tf_op jit(solution)/shard_map/ppermute | solution.py:18
  264.1 25.4 %collective-permute-start.1 = (bf16[4,24,1024]{2,1,0:T(8,128)(2,1)S(1)}, bf16[4,24,1024]{2,1,0:T(8,128)(2,1)S(1)}, u32[]{:S(2)}, u32[]{:S(2)}) collective-permute-start(bf16[4,24,1024]{2,1,0:T(8,128)(2,1)S(1)} %bitcast.71), channel_id=1, source_target_pairs={{2,0},{4,2},{6,4},{8,6},{10,8},{12,10},{14,12},{16,14},{18,16},{20... | collective-permute-start | bytes 589832 | tf_op jit(solution)/shard_map/ppermute | solution.py:19
  269.0 33.3 %copy-start.2 = (bf16[128,24,1024]{2,1,0:T(8,128)(2,1)}, bf16[128,24,1024]{2,1,0:T(8,128)(2,1)S(1)}, u32[]{:S(2)}) copy-start(bf16[128,24,1024]{2,1,0:T(8,128)(2,1)S(1)} %broadcast_select_fusion.1) | copy-start | bytes 18874372
  269.0 7.6 %copy-start.5 = (bf16[128,16,24]{2,1,0:T(8,128)(2,1)S(1)}, bf16[128,16,24]{2,1,0:T(8,128)(2,1)}, u32[]{:S(2)}) copy-start(bf16[128,16,24]{2,1,0:T(8,128)(2,1)} %copy.43) | copy-start | bytes 294916
  276.6 4.2 %copy-start.6 = (bf16[128,16,24]{2,1,0:T(8,128)(2,1)S(1)}, bf16[128,16,24]{2,1,0:T(8,128)(2,1)}, u32[]{:S(2)}) copy-start(bf16[128,16,24]{2,1,0:T(8,128)(2,1)} %copy.45) | copy-start | bytes 294916
  285.1 4.3 %copy-start.7 = (bf16[128,16,24]{2,1,0:T(8,128)(2,1)S(1)}, bf16[128,16,24]{2,1,0:T(8,128)(2,1)}, u32[]{:S(2)}) copy-start(bf16[128,16,24]{2,1,0:T(8,128)(2,1)} %copy.53) | copy-start | bytes 294916
  289.5 4.3 %copy-start.8 = (bf16[128,16,24]{2,1,0:T(8,128)(2,1)S(1)}, bf16[128,16,24]{2,1,0:T(8,128)(2,1)}, u32[]{:S(2)}) copy-start(bf16[128,16,24]{2,1,0:T(8,128)(2,1)} %copy.55) | copy-start | bytes 294916
  293.8 4.3 %copy-start.9 = (bf16[128,16,24]{2,1,0:T(8,128)(2,1)S(1)}, bf16[128,16,24]{2,1,0:T(8,128)(2,1)}, u32[]{:S(2)}) copy-start(bf16[128,16,24]{2,1,0:T(8,128)(2,1)} %copy.57) | copy-start | bytes 294916
  306.6 55.5 %copy-start.1 = (f32[256,256]{1,0:T(8,128)S(1)}, f32[256,256]{1,0:T(8,128)}, u32[]{:S(2)}) copy-start(f32[256,256]{1,0:T(8,128)} %param.11) | copy-start | bytes 786436
Sparse Core Ops, SparseCore 0:
  9.5 11.4 all-gather.3
  26.0 192.1 all-gather.5
  354.3 6.1 reduce-scatter.3
